TPU v7x, 32 devices: a whole 2x2x4 slice. The times are simulated.
32 devices in a mesh: tm: 16 (over z, y, x), row: 2 (over core).
Axes of the slice: x: 2, y: 2, z: 4, core: 2. Of those that a mesh axis runs over, the one named last changes fastest.
Arguments:
- initial: float32 [1024], replicated, may hold values from -6 to 6
- dynamics: float32 [1024, 1024], replicated, may hold values from -0.009765625 to 0.009765625
- obs_rows: bfloat16 [32768, 1024], P('tm', 'row'), may hold values from -0.1875 to 0.1875
- obs_values: bfloat16 [32768], P('tm'), may hold values from -6 to 6
- obs_slab: int32 [32768, 1], P('tm'), may hold values from 0 to 31; in each aligned block of 2048 rows (0 to 2047, 2048 to 4095, ...) at most 64 rows name the same one
Outputs:
- states: float32 [32, 1024], P('tm', 'row')
Inputs may be any that keep to these rules, and one draw needn't show every extreme that they name: `obs_slab`: within the rows ingested by one index of tm, no slab is named by more than 64 rows, a bound that some block reaches of them.
All inputs are finite; a program needn't handle non-finite values.
Results may differ from a plain program's by a relative error of at most 0.0003.
Values may be sent and summed in bfloat16 or wider, within the bound.
A program may use at most 128 MiB of HBM per device.

v0:
```python
import jax
import jax.numpy as jnp
from jax import lax
from jax.experimental import pallas as pl
from jax.experimental.pallas import tpu as pltpu
from jax.sharding import PartitionSpec as P

CAP = 64
LANES = 128
MESH = pl.DeviceIdType.MESH

sigma_gain = 0.3


def visit(own, turn, total):
    if total & (total - 1):
        return lax.rem(own + turn, total)
    if total == 4:
        turn = ((turn & 1) << 1) | (turn >> 1)
    return own ^ turn


def chip_at(place):
    turn = place & 3
    turn = jnp.where((place >> 2) & 1 == 1, 3 - turn, turn)
    return (place - (place & 3)) + jnp.where(turn < 2, turn, 5 - turn)


def place_of(chip):
    turn = chip & 3
    turn = jnp.where(turn < 2, turn, 5 - turn)
    return (chip - (chip & 3)) + jnp.where((chip >> 2) & 1 == 1, 3 - turn, turn)


def observer_kernel(
    target_ref, rows_ref, values_ref, dynamics_ref, start_ref, out_ref,
    sent, sent_values, slot_ref, got, got_values, dynamics, dyn_high, dyn_low, turned, gain, moment,
    high_ref, low_ref, b_ref, perm, high_got, low_got, b_got, came, went, back, offset, owner_ref,
    row_send, row_recv, value_send, value_recv, own_sem, send_sem, recv_sem, tile_send, tile_recv, out_send, out_recv,
):
    time_devs, row_devs = lax.axis_size("tm"), lax.axis_size("row")
    t, r = lax.axis_index("tm"), lax.axis_index("row")
    slabs = time_devs * row_devs
    last = time_devs - 1
    place_here = place_of(t)
    after = chip_at(jnp.minimum(place_here + 1, last))
    me = t * row_devs + r
    partner = (t, 1 - r)
    count, local = rows_ref.shape
    width = local * row_devs
    subs = width // LANES
    tile = 256
    tiles = width // tile
    block = 256
    share = block // CAP
    blocks = slabs // share

    def device(slab):
        return (slab // row_devs, lax.rem(slab, row_devs))

    barrier = pltpu.get_barrier_semaphore()

    def greet(slab, _):
        @pl.when(slab != me)
        def _():
            pl.semaphore_signal(barrier, inc=1, device_id=device(slab), device_id_type=MESH)

        return 0

    lax.fori_loop(0, slabs, greet, 0)
    fetch = pltpu.make_async_copy(dynamics_ref, dynamics, own_sem.at[2])
    fetch.start()

    before = (
        lax.broadcasted_iota(jnp.int32, (block, block), 0)
        < lax.broadcasted_iota(jnp.int32, (block, block), 1)
    ).astype(jnp.float32).astype(jnp.bfloat16)
    slab_of = lax.broadcasted_iota(jnp.int32, (slabs, block), 0)
    carry = (slab_of[:, :1] * CAP).astype(jnp.float32)
    pair = row_devs.bit_length() - 1
    target = target_ref[...]
    owner_ref[...] = (chip_at(target >> pair) << pair) + (target & (row_devs - 1))
    for start in range(0, count, block):
        named = (owner_ref[:, start : start + block] == slab_of).astype(jnp.float32)
        ahead = jnp.dot(named.astype(jnp.bfloat16), before, preferred_element_type=jnp.float32)
        slot = jnp.sum(named * (ahead + carry), axis=0, keepdims=True)
        slot_ref[:, start : start + block] = slot.astype(jnp.int32)
        carry = carry + jnp.sum(named, axis=1, keepdims=True)

    values = jnp.broadcast_to(values_ref[...].astype(jnp.float32), (8, count)).astype(jnp.bfloat16)
    sent_values[...] = jnp.zeros_like(sent_values)

    def landing(source):
        rows = pl.ds(pl.multiple_of(source // row_devs * CAP, CAP), CAP)
        cols = pl.ds(pl.multiple_of(lax.rem(source, row_devs) * local, local), local)
        return got.at[rows, cols]

    def copies(slab, source):
        rows = pltpu.make_async_remote_copy(
            src_ref=sent.at[slab], dst_ref=landing(source),
            send_sem=row_send.at[slab], recv_sem=row_recv.at[source],
            device_id=device(slab), device_id_type=MESH,
        )
        tags = pltpu.make_async_remote_copy(
            src_ref=sent_values.at[slab], dst_ref=got_values.at[source],
            send_sem=value_send.at[slab], recv_sem=value_recv.at[source],
            device_id=device(slab), device_id_type=MESH,
        )
        return rows, tags

    keep = (
        pltpu.make_async_copy(sent.at[me], landing(me), own_sem.at[0]),
        pltpu.make_async_copy(sent_values.at[me], got_values.at[me], own_sem.at[1]),
    )

    def place(at):
        first = at * share
        wanted = lax.broadcasted_iota(jnp.int32, (block, count), 0) + first * CAP
        pick = (wanted == slot_ref[...]).astype(jnp.float32).astype(jnp.bfloat16)
        rows = jnp.dot(pick, rows_ref[...], preferred_element_type=jnp.float32).astype(jnp.bfloat16)
        tags = lax.dot_general(
            values, pick, (((1,), (1,)), ((), ())), preferred_element_type=jnp.float32
        )[:1]
        for inner in range(share):
            sent[first + inner] = rows[inner * CAP : (inner + 1) * CAP]
            sent_values[first + inner, :, :CAP] = tags[:, inner * CAP : (inner + 1) * CAP]

    def send(at):
        for inner in range(share):
            slab = at * share + inner

            @pl.when(slab != me)
            def _():
                for copy in copies(slab, me):
                    copy.start()

            @pl.when(slab == me)
            def _():
                for copy in keep:
                    copy.start()

    mine = me // share
    layered = 2
    place(mine)
    pl.semaphore_wait(barrier, slabs - 1)
    send(mine)

    def step(turn, _):
        layer, within = turn // layered, lax.rem(turn, layered)
        at = visit(mine // layered, layer, blocks // layered) * layered
        at = at + lax.rem(mine + within, layered)
        place(at)
        send(at)
        return 0

    lax.fori_loop(1, blocks, step, 0)

    fetch.wait()

    def divide(k, _):
        rows = pl.ds(pl.multiple_of(k * LANES, LANES), LANES)
        high = dynamics[rows, :].astype(jnp.bfloat16)
        dyn_high[rows, :] = high
        dyn_low[rows, :] = (dynamics[rows, :] - high.astype(jnp.float32)).astype(jnp.bfloat16)
        return 0

    lax.fori_loop(0, subs, divide, 0)
    gain[...] = jnp.zeros_like(gain)
    moment[...] = jnp.zeros_like(moment)

    chips = block // CAP
    groups = time_devs // chips
    nearest = t // chips

    def gather(turn, _):
        at = visit(nearest, turn, groups)

        def arrive(source, _):
            @pl.when(source != me)
            def _():
                for copy in copies(source, source):
                    copy.wait_recv()

            @pl.when(source == me)
            def _():
                for copy in keep:
                    copy.wait()

            return 0

        lax.fori_loop(at * chips * row_devs, (at + 1) * chips * row_devs, arrive, 0)
        own = pl.ds(pl.multiple_of(at * block, block), block)
        rows = got[own, :]
        turned[...] = rows.T
        tags = jnp.concatenate(
            [got_values[(at * chips + k) * row_devs][:, :CAP] for k in range(chips)], axis=1
        )
        tags = jnp.broadcast_to(tags, (8, block)).astype(jnp.bfloat16)
        moment[...] += jnp.dot(tags, rows, preferred_element_type=jnp.float32)

        def column(k, _):
            cols = pl.ds(pl.multiple_of(k * tile, tile), tile)
            seen = (
                got[own, cols].astype(jnp.float32)
                + jnp.dot(got[own, :], dyn_high[:, cols], preferred_element_type=jnp.float32)
                + jnp.dot(got[own, :], dyn_low[:, cols], preferred_element_type=jnp.float32)
            )
            high = seen.astype(jnp.bfloat16)
            low = (seen - high.astype(jnp.float32)).astype(jnp.bfloat16)
            gain[:, cols] += jnp.dot(
                turned[...], high, preferred_element_type=jnp.float32
            ) + jnp.dot(turned[...], low, preferred_element_type=jnp.float32)
            return 0

        lax.fori_loop(0, tiles, column, 0)
        return 0

    lax.fori_loop(0, groups, gather, 0)

    def push(source, target, index, peer):
        return pltpu.make_async_remote_copy(
            src_ref=source, dst_ref=target, send_sem=send_sem.at[index],
            recv_sem=recv_sem.at[index], device_id=peer, device_id_type=MESH,
        )

    lend = push(b_ref, b_got, 0, partner)
    onward = push(went, came, 2, (after, 1))
    aside = pltpu.make_async_remote_copy(
        src_ref=went, dst_ref=came, send_sem=send_sem.at[3],
        recv_sem=recv_sem.at[2], device_id=(after, 0), device_id_type=MESH,
    )

    def part(k):
        cols = pl.ds(pl.multiple_of(k * tile, tile), tile)
        return [
            pltpu.make_async_remote_copy(
                src_ref=source.at[:, cols], dst_ref=target.at[:, cols],
                send_sem=tile_send.at[index, k], recv_sem=tile_recv.at[index, k],
                device_id=partner, device_id_type=MESH,
            )
            for index, (source, target) in enumerate(((high_ref, high_got), (low_ref, low_got)))
        ]

    for sub in range(subs):
        b_ref[sub : sub + 1, :] = sigma_gain * moment[:1, sub * LANES : (sub + 1) * LANES]

    @pl.when(r == 0)
    def _():
        lend.start()

    def settle(k, _):
        cols = pl.ds(pl.multiple_of(k * tile, tile), tile)
        for sub in range(subs):
            own = slice(sub * LANES, (sub + 1) * LANES)
            diagonal = (
                lax.broadcasted_iota(jnp.int32, (LANES, tile), 0) + sub * LANES
                == lax.broadcasted_iota(jnp.int32, (LANES, tile), 1) + k * tile
            ).astype(jnp.float32)
            whole = diagonal + dynamics[own, cols] - sigma_gain * gain[own, cols]
            high = whole.astype(jnp.bfloat16)
            high_ref[own, cols] = high
            low_ref[own, cols] = (whole - high.astype(jnp.float32)).astype(jnp.bfloat16)
            perm[:, sub, cols] = whole

        @pl.when(r == 0)
        def _():
            for copy in part(k):
                copy.start()

        return 0

    lax.fori_loop(0, tiles, settle, 0)

    lane = lax.broadcasted_iota(jnp.int32, (subs, LANES), 1)
    group = 16

    def apply(vector):
        pieces = [jnp.broadcast_to(vector[k : k + 1, :], (subs, LANES)) for k in range(subs)]

        def rows(step, total):
            for inner in range(group):
                g = step * group + inner
                part = perm[g, :, 0:LANES] * pieces[0]
                for k in range(1, subs):
                    part = part + perm[g, :, k * LANES : (k + 1) * LANES] * pieces[k]
                total = jnp.where(lane == g, jnp.sum(part, axis=1, keepdims=True), total)
            return total

        return lax.fori_loop(0, LANES // group, rows, jnp.zeros((subs, LANES), jnp.float32))

    offset[...] = b_ref[...]

    @pl.when(r == 1)
    def _():
        lend.wait_recv()
        offset[...] = apply(b_got[...]) + b_ref[...]

        def compose(k, _):
            for copy in part(k):
                copy.wait_recv()
            cols = pl.ds(pl.multiple_of(k * tile, tile), tile)
            high, low = high_got[:, cols], low_got[:, cols]
            whole = (
                jnp.dot(high_ref[...], high, preferred_element_type=jnp.float32)
                + jnp.dot(high_ref[...], low, preferred_element_type=jnp.float32)
                + jnp.dot(low_ref[...], high, preferred_element_type=jnp.float32)
            )
            for sub in range(subs):
                perm[:, sub, cols] = whole[sub * LANES : (sub + 1) * LANES, :]
            return 0

        lax.fori_loop(0, tiles, compose, 0)

    @pl.when(r == 0)
    def _():
        lend.wait_send()

        def drain(k, _):
            for copy in part(k):
                copy.wait_send()
            return 0

        lax.fori_loop(0, tiles, drain, 0)

    @pl.when(place_here == 0)
    def _():
        came[...] = start_ref[...]

    @pl.when(place_here > 0)
    def _():
        onward.wait_recv()

    went[...] = apply(came[...]) + offset[...]
    passing = (r == 1) & (place_here < last)

    @pl.when(passing)
    def _():
        onward.start()
        aside.start()

    stays = place_here == t

    def report(core, sender):
        return pltpu.make_async_remote_copy(
            src_ref=went, dst_ref=back.at[sender], send_sem=out_send.at[core],
            recv_sem=out_recv.at[sender], device_id=(place_here, core), device_id_type=MESH,
        )

    for core in range(2):
        @pl.when(jnp.logical_not(stays & (r == core)))
        def _():
            report(core, r).start()

        @pl.when(stays & (r == core))
        def _():
            back[core] = went[...]

    for core in range(2):
        @pl.when(jnp.logical_not(stays & (r == core)))
        def _():
            report(core, core).wait_recv()
            report(core, r).wait_send()

    half = subs // 2

    @pl.when(r == 0)
    def _():
        out_ref[0] = back[0, :half, :]
        out_ref[1] = back[1, :half, :]

    @pl.when(r == 1)
    def _():
        out_ref[0] = back[0, half:, :]
        out_ref[1] = back[1, half:, :]

    @pl.when(passing)
    def _():
        onward.wait_send()
        aside.wait_send()

    def finish(slab, _):
        @pl.when(slab != me)
        def _():
            for copy in copies(slab, slab):
                copy.wait_send()

        return 0

    lax.fori_loop(0, slabs, finish, 0)


def body(initial, dynamics, obs_rows, obs_values, obs_slab):
    time_devs = lax.axis_size("tm")
    row_devs = lax.axis_size("row")
    width = dynamics.shape[1]
    count, local = obs_rows.shape
    slabs = time_devs * row_devs
    subs = width // LANES
    tiles = width // 256
    vmem = pl.BlockSpec(memory_space=pltpu.VMEM)
    small = pltpu.VMEM((subs, LANES), jnp.float32)
    square = pltpu.VMEM((width, width), jnp.bfloat16)
    square32 = pltpu.VMEM((width, width), jnp.float32)
    sems = pltpu.SemaphoreType.DMA((slabs,))
    states = pl.pallas_call(
        observer_kernel,
        out_shape=jax.ShapeDtypeStruct((2, subs // 2, LANES), jnp.float32),
        in_specs=[vmem, vmem, vmem, pl.BlockSpec(memory_space=pl.ANY), vmem],
        out_specs=vmem,
        scratch_shapes=[
            pltpu.VMEM((slabs, CAP, local), jnp.bfloat16),
            pltpu.VMEM((slabs, 1, LANES), jnp.float32),
            pltpu.VMEM((1, count), jnp.int32),
            pltpu.VMEM((time_devs * CAP, width), jnp.bfloat16),
            pltpu.VMEM((slabs, 1, LANES), jnp.float32),
            square32,
            square,
            square,
            pltpu.VMEM((width, 256), jnp.bfloat16),
            square32,
            pltpu.VMEM((8, width), jnp.float32),
            square,
            square,
            small,
            pltpu.VMEM((LANES, subs, width), jnp.float32),
            square,
            square,
            small,
            small,
            small,
            pltpu.VMEM((2, subs, LANES), jnp.float32),
            small,
            pltpu.VMEM((1, count), jnp.int32),
            sems,
            sems,
            sems,
            sems,
            pltpu.SemaphoreType.DMA((3,)),
            pltpu.SemaphoreType.DMA((4,)),
            pltpu.SemaphoreType.DMA((3,)),
            pltpu.SemaphoreType.DMA((2, tiles)),
            pltpu.SemaphoreType.DMA((2, tiles)),
            pltpu.SemaphoreType.DMA((2,)),
            pltpu.SemaphoreType.DMA((2,)),
        ],
        compiler_params=pltpu.CompilerParams(
            collective_id=0, has_side_effects=True, vmem_limit_bytes=60 << 20
        ),
        name="observer",
    )(
        obs_slab.reshape(1, -1),
        obs_rows,
        obs_values.reshape(1, -1),
        dynamics,
        initial.reshape(subs, LANES),
    )
    return states.reshape(2, width // 2)


def solution(mesh):
    placed = (P(), P(), P("tm", "row"), P("tm"), P("tm", None))
    return jax.shard_map(
        body, mesh=mesh, in_specs=placed, out_specs=P("tm", "row"), check_vma=False
    )
```

profile of v0, /device:TPU:29, one launch (start us, length us, event | category | flops | bytes accessed | tf_op | source)
XLA Modules:
  0.0 115.7 jit_solution(6208910412570658659)
XLA Ops:
  0.0 1.3 %reshape.13.values_ref = bf16[1,2048]{1,0:T(2,128)(2,1)} reshape(bf16[2048]{0:T(1024)(128)(2,1)} %param.8) | data formatting | bytes 8192 | tf_op jit(solution)/shard_map/reshape | solution.py:453
  1.3 113.2 %observer.1 = f32[2,4,128]{2,1,0:T(4,128)} custom-call(s32[1,2048]{1,0:T(1,128)} %bitcast.7, bf16[2048,512]{1,0:T(8,128)(2,1)} %rows_ref.1, bf16[1,2048]{1,0:T(2,128)(2,1)} %reshape.13.values_ref, f32[1024,1024]{1,0:T(8,128)} %dynamics_ref.1, f32[8,128]{1,0:T(8,128)} %bitcast.8), custom_call_target="tpu_custom_call" | custom-call | tf_op jit(solution)/shard_map/observer/pallas_call | solution.py:405
  114.5 1.3 %copy.8 = f32[1,2,4,128]{3,1,2,0:T(2,128)} copy(f32[1,2,4,128]{3,2,1,0:T(4,128)} %bitcast.6) | data formatting | bytes 8192
where the time goes:
time: 118 us; the launch traced here: 116 us
  Pallas kernels  113 us (96%)
  local copies, waits for them, and re-layouts  2.55 us (2%)
    pallas_call x1, Pallas kernels, body(): pl.pallas_call(observer_kernel, out_shape=jax.ShapeDtypeStruct((2, subs /...  113 us

commit v1 on v0

--- a/solution.py
+++ b/solution.py
@@ -20,31 +20,36 @@
     return own ^ turn
 
 
-def chip_at(place):
-    turn = place & 3
-    turn = jnp.where((place >> 2) & 1 == 1, 3 - turn, turn)
-    return (place - (place & 3)) + jnp.where(turn < 2, turn, 5 - turn)
-
-
-def place_of(chip):
-    turn = chip & 3
-    turn = jnp.where(turn < 2, turn, 5 - turn)
-    return (chip - (chip & 3)) + jnp.where((chip >> 2) & 1 == 1, 3 - turn, turn)
+def chip_at(place, planes):
+    column = place // planes
+    depth = lax.rem(place, planes)
+    depth = jnp.where(column & 1 == 1, depth, planes - 1 - depth)
+    turn = (column + 3) & 3
+    return depth * 4 + (turn ^ (turn >> 1))
+
+
+def place_of(chip, planes):
+    depth, turn = chip // 4, chip & 3
+    column = ((turn ^ (turn >> 1)) + 1) & 3
+    depth = jnp.where(column & 1 == 1, depth, planes - 1 - depth)
+    return column * planes + depth
 
 
 def observer_kernel(
     target_ref, rows_ref, values_ref, dynamics_ref, start_ref, out_ref,
     sent, sent_values, slot_ref, got, got_values, dynamics, dyn_high, dyn_low, turned, gain, moment,
-    high_ref, low_ref, b_ref, perm, high_got, low_got, b_got, came, went, back, offset, owner_ref,
+    high_ref, low_ref, b_ref, perm, high_got, low_got, b_got, came, went, back, offset,
     row_send, row_recv, value_send, value_recv, own_sem, send_sem, recv_sem, tile_send, tile_recv, out_send, out_recv,
 ):
     time_devs, row_devs = lax.axis_size("tm"), lax.axis_size("row")
     t, r = lax.axis_index("tm"), lax.axis_index("row")
     slabs = time_devs * row_devs
     last = time_devs - 1
-    place_here = place_of(t)
-    after = chip_at(jnp.minimum(place_here + 1, last))
-    me = t * row_devs + r
+    planes = time_devs // 4
+    place_here = place_of(t, planes)
+    after = chip_at(jnp.minimum(place_here + 1, last), planes)
+    me = place_here * row_devs + r
+    here = t * row_devs + r
     partner = (t, 1 - r)
     count, local = rows_ref.shape
     width = local * row_devs
@@ -56,7 +61,7 @@
     blocks = slabs // share
 
     def device(slab):
-        return (slab // row_devs, lax.rem(slab, row_devs))
+        return (chip_at(slab // row_devs, planes), lax.rem(slab, row_devs))
 
     barrier = pltpu.get_barrier_semaphore()
 
@@ -77,11 +82,8 @@
     ).astype(jnp.float32).astype(jnp.bfloat16)
     slab_of = lax.broadcasted_iota(jnp.int32, (slabs, block), 0)
     carry = (slab_of[:, :1] * CAP).astype(jnp.float32)
-    pair = row_devs.bit_length() - 1
-    target = target_ref[...]
-    owner_ref[...] = (chip_at(target >> pair) << pair) + (target & (row_devs - 1))
     for start in range(0, count, block):
-        named = (owner_ref[:, start : start + block] == slab_of).astype(jnp.float32)
+        named = (target_ref[:, start : start + block] == slab_of).astype(jnp.float32)
         ahead = jnp.dot(named.astype(jnp.bfloat16), before, preferred_element_type=jnp.float32)
         slot = jnp.sum(named * (ahead + carry), axis=0, keepdims=True)
         slot_ref[:, start : start + block] = slot.astype(jnp.int32)
@@ -109,8 +111,8 @@
         return rows, tags
 
     keep = (
-        pltpu.make_async_copy(sent.at[me], landing(me), own_sem.at[0]),
-        pltpu.make_async_copy(sent_values.at[me], got_values.at[me], own_sem.at[1]),
+        pltpu.make_async_copy(sent.at[me], landing(here), own_sem.at[0]),
+        pltpu.make_async_copy(sent_values.at[me], got_values.at[here], own_sem.at[1]),
     )
 
     def place(at):
@@ -125,13 +127,24 @@
             sent[first + inner] = rows[inner * CAP : (inner + 1) * CAP]
             sent_values[first + inner, :, :CAP] = tags[:, inner * CAP : (inner + 1) * CAP]
 
-    def send(at):
+    column_blocks = planes * row_devs // share
+    depth = t // 4
+
+    def order(turn):
+        column = turn // column_blocks
+        along = jnp.where(column & 1 == 1, depth, planes - 1 - depth)
+        own = along * row_devs // share
+        return column * column_blocks + (own ^ lax.rem(turn, column_blocks)), along
+
+    def send(turn):
+        at, along = order(turn)
+        key = lax.rem(along * row_devs, share) + r
         for inner in range(share):
-            slab = at * share + inner
+            slab = at * share + (key ^ inner)
 
             @pl.when(slab != me)
             def _():
-                for copy in copies(slab, me):
+                for copy in copies(slab, here):
                     copy.start()
 
             @pl.when(slab == me)
@@ -139,18 +152,13 @@
                 for copy in keep:
                     copy.start()
 
-    mine = me // share
-    layered = 2
-    place(mine)
+    place(order(0)[0])
     pl.semaphore_wait(barrier, slabs - 1)
-    send(mine)
+    send(0)
 
     def step(turn, _):
-        layer, within = turn // layered, lax.rem(turn, layered)
-        at = visit(mine // layered, layer, blocks // layered) * layered
-        at = at + lax.rem(mine + within, layered)
-        place(at)
-        send(at)
+        place(order(turn)[0])
+        send(turn)
         return 0
 
     lax.fori_loop(1, blocks, step, 0)
@@ -176,12 +184,12 @@
         at = visit(nearest, turn, groups)
 
         def arrive(source, _):
-            @pl.when(source != me)
+            @pl.when(source != here)
             def _():
-                for copy in copies(source, source):
+                for copy in copies(me, source):
                     copy.wait_recv()
 
-            @pl.when(source == me)
+            @pl.when(source == here)
             def _():
                 for copy in keep:
                     copy.wait()
@@ -381,7 +389,7 @@
     def finish(slab, _):
         @pl.when(slab != me)
         def _():
-            for copy in copies(slab, slab):
+            for copy in copies(slab, here):
                 copy.wait_send()
 
         return 0
@@ -430,7 +438,6 @@
             small,
             pltpu.VMEM((2, subs, LANES), jnp.float32),
             small,
-            pltpu.VMEM((1, count), jnp.int32),
             sems,
             sems,
             sems,

time: 118 us -> 111 us (0.941); the launches traced: 116 us -> 111 us
  Pallas kernels: 113 us -> 108 us
    pallas_call x1, Pallas kernels: 113 us -> 108 us  [body(): pl.pallas_call(observer_kernel, out_shape=jax.ShapeDtypeStruct((2, subs /...]
where the time goes in v1:
time: 111 us
  Pallas kernels  108 us (97%)
  local copies, waits for them, and re-layouts  2.55 us (2%)
    pallas_call x1, Pallas kernels, body(): pl.pallas_call(observer_kernel, out_shape=jax.ShapeDtypeStruct((2, subs /...  108 us

profile of v1, /device:TPU:29, one launch (start us, length us, event | category | flops | bytes accessed | tf_op | source)
XLA Modules:
  0.0 110.8 jit_solution(4723988851638516727)
XLA Ops:
  0.0 1.3 %reshape.13.values_ref = bf16[1,2048]{1,0:T(2,128)(2,1)} reshape(bf16[2048]{0:T(1024)(128)(2,1)} %param.8) | data formatting | bytes 8192 | tf_op jit(solution)/shard_map/reshape | solution.py:460
  1.3 108.2 %observer.1 = f32[2,4,128]{2,1,0:T(4,128)} custom-call(s32[1,2048]{1,0:T(1,128)} %bitcast.7, bf16[2048,512]{1,0:T(8,128)(2,1)} %rows_ref.1, bf16[1,2048]{1,0:T(2,128)(2,1)} %reshape.13.values_ref, f32[1024,1024]{1,0:T(8,128)} %dynamics_ref.1, f32[8,128]{1,0:T(8,128)} %bitcast.8), custom_call_target="tpu_custom_call" | custom-call | tf_op jit(solution)/shard_map/observer/pallas_call | solution.py:413
  109.5 1.3 %copy.8 = f32[1,2,4,128]{3,1,2,0:T(2,128)} copy(f32[1,2,4,128]{3,2,1,0:T(4,128)} %bitcast.6) | data formatting | bytes 8192

commit v2 on v1

v2 whole, which is shorter than its diff:
```python
import jax
import jax.numpy as jnp
from jax import lax
from jax.experimental import pallas as pl
from jax.experimental.pallas import tpu as pltpu
from jax.sharding import PartitionSpec as P

CAP = 64
LANES = 128
MESH = pl.DeviceIdType.MESH

sigma_gain = 0.3


def visit(own, turn, total):
    if total & (total - 1):
        return lax.rem(own + turn, total)
    return own ^ turn


def chip_at(place, planes):
    column = place // planes
    depth = lax.rem(place, planes)
    depth = jnp.where(column & 1 == 1, depth, planes - 1 - depth)
    turn = (column + 3) & 3
    return depth * 4 + (turn ^ (turn >> 1))


def place_of(chip, planes):
    depth, turn = chip // 4, chip & 3
    column = ((turn ^ (turn >> 1)) + 1) & 3
    depth = jnp.where(column & 1 == 1, depth, planes - 1 - depth)
    return column * planes + depth


def observer_kernel(
    target_ref, rows_hbm, values_ref, dynamics_ref, start_ref, out_ref,
    rows_ref, values_row, sent, sent_values, slot_ref, got, got_values, dynamics, dyn_high, turned, gain, moment,
    whole, left, lent_left, right, lent_right, b_ref, b_got, came, went, middle, back,
    row_send, row_recv, value_send, value_recv, own_sem, lend_sem, tile_send, tile_recv, pass_send, pass_recv,
    out_send, out_recv,
):
    time_devs, row_devs = lax.axis_size("tm"), lax.axis_size("row")
    t, r = lax.axis_index("tm"), lax.axis_index("row")
    slabs = time_devs * row_devs
    last = time_devs - 1
    planes = time_devs // 4
    place_here = place_of(t, planes)
    after = chip_at(jnp.minimum(place_here + 1, last), planes)
    me = place_here * row_devs + r
    here = t * row_devs + r
    partner = (t, 1 - r)
    count, local = rows_ref.shape
    width = local * row_devs
    subs = width // LANES
    tile = 256
    tiles = width // tile
    block = 256
    share = block // CAP
    blocks = slabs // share

    def device(slab):
        return (chip_at(slab // row_devs, planes), lax.rem(slab, row_devs))

    barrier = pltpu.get_barrier_semaphore()

    def greet(slab, _):
        @pl.when(slab != me)
        def _():
            pl.semaphore_signal(barrier, inc=1, device_id=device(slab), device_id_type=MESH)

        return 0

    lax.fori_loop(0, slabs, greet, 0)
    rows_in = pltpu.make_async_copy(rows_hbm, rows_ref, own_sem.at[3])
    rows_in.start()
    fetch = pltpu.make_async_copy(dynamics_ref, dynamics, own_sem.at[2])
    fetch.start()

    before = (
        lax.broadcasted_iota(jnp.int32, (block, block), 0)
        < lax.broadcasted_iota(jnp.int32, (block, block), 1)
    ).astype(jnp.float32).astype(jnp.bfloat16)
    slab_of = lax.broadcasted_iota(jnp.int32, (slabs, block), 0)
    carry = (slab_of[:, :1] * CAP).astype(jnp.float32)
    for start in range(0, count, block):
        named = (target_ref[:, start : start + block] == slab_of).astype(jnp.float32)
        ahead = jnp.dot(named.astype(jnp.bfloat16), before, preferred_element_type=jnp.float32)
        slot = jnp.sum(named * (ahead + carry), axis=0, keepdims=True)
        slot_ref[:, start : start + block] = slot.astype(jnp.int32)
        carry = carry + jnp.sum(named, axis=1, keepdims=True)

    spread = values_ref[...].astype(jnp.float32)
    for line in range(count // LANES):
        values_row[:, line * LANES : (line + 1) * LANES] = spread[line : line + 1, :]
    values = jnp.broadcast_to(values_row[...], (8, count)).astype(jnp.bfloat16)
    sent_values[...] = jnp.zeros_like(sent_values)

    def landing(source):
        rows = pl.ds(pl.multiple_of(source // row_devs * CAP, CAP), CAP)
        cols = pl.ds(pl.multiple_of(lax.rem(source, row_devs) * local, local), local)
        return got.at[rows, cols]

    def copies(slab, source):
        rows = pltpu.make_async_remote_copy(
            src_ref=sent.at[slab], dst_ref=landing(source),
            send_sem=row_send.at[slab], recv_sem=row_recv.at[source],
            device_id=device(slab), device_id_type=MESH,
        )
        tags = pltpu.make_async_remote_copy(
            src_ref=sent_values.at[slab], dst_ref=got_values.at[source],
            send_sem=value_send.at[slab], recv_sem=value_recv.at[source],
            device_id=device(slab), device_id_type=MESH,
        )
        return rows, tags

    keep = (
        pltpu.make_async_copy(sent.at[me], landing(here), own_sem.at[0]),
        pltpu.make_async_copy(sent_values.at[me], got_values.at[here], own_sem.at[1]),
    )

    def place(at):
        first = at * share
        wanted = lax.broadcasted_iota(jnp.int32, (block, count), 0) + first * CAP
        pick = (wanted == slot_ref[...]).astype(jnp.float32).astype(jnp.bfloat16)
        rows = jnp.dot(pick, rows_ref[...], preferred_element_type=jnp.float32).astype(jnp.bfloat16)
        tags = lax.dot_general(
            values, pick, (((1,), (1,)), ((), ())), preferred_element_type=jnp.float32
        )[:1]
        for inner in range(share):
            sent[first + inner] = rows[inner * CAP : (inner + 1) * CAP]
            sent_values[first + inner, :, :CAP] = tags[:, inner * CAP : (inner + 1) * CAP]

    column_blocks = planes * row_devs // share
    depth = t // 4

    def order(turn):
        column = turn // column_blocks
        along = jnp.where(column & 1 == 1, depth, planes - 1 - depth)
        own = along * row_devs // share
        return column * column_blocks + (own ^ lax.rem(turn, column_blocks)), along

    def send(turn):
        at, along = order(turn)
        key = lax.rem(along * row_devs, share) + r
        for inner in range(share):
            slab = at * share + (key ^ inner)

            @pl.when(slab != me)
            def _():
                rows, tags = copies(slab, here)
                rows.start()

                @pl.when(r == 0)
                def _():
                    tags.start()

            @pl.when(slab == me)
            def _():
                for copy in keep:
                    copy.start()

    rows_in.wait()
    place(order(0)[0])
    pl.semaphore_wait(barrier, slabs - 1)
    send(0)

    def step(turn, _):
        place(order(turn)[0])
        send(turn)
        return 0

    lax.fori_loop(1, blocks, step, 0)

    fetch.wait()

    def divide(k, _):
        rows = pl.ds(pl.multiple_of(k * LANES, LANES), LANES)
        high = dynamics[rows, :].astype(jnp.bfloat16)
        dyn_high[rows, :] = high
        return 0

    lax.fori_loop(0, subs, divide, 0)
    gain[...] = jnp.zeros_like(gain)
    moment[...] = jnp.zeros_like(moment)

    chips = block // CAP
    groups = time_devs // chips
    nearest = t // chips

    def gather(turn, _):
        at = visit(nearest, turn, groups)

        def arrive(source, _):
            @pl.when(source != here)
            def _():
                rows, tags = copies(me, source)
                rows.wait_recv()

                @pl.when(lax.rem(source, row_devs) == 0)
                def _():
                    tags.wait_recv()

            @pl.when(source == here)
            def _():
                for copy in keep:
                    copy.wait()

            return 0

        lax.fori_loop(at * chips * row_devs, (at + 1) * chips * row_devs, arrive, 0)
        own = pl.ds(pl.multiple_of(at * block, block), block)
        rows = got[own, :]
        flipped = rows.T
        turned[:, :block] = flipped
        turned[:, block:] = flipped
        tags = jnp.concatenate(
            [got_values[(at * chips + k) * row_devs][:, :CAP] for k in range(chips)], axis=1
        )
        tags = jnp.broadcast_to(tags, (8, block)).astype(jnp.bfloat16)
        moment[...] += jnp.dot(tags, rows, preferred_element_type=jnp.float32)

        def column(k, _):
            cols = pl.ds(pl.multiple_of(k * tile, tile), tile)
            moved = jnp.dot(got[own, :], dyn_high[:, cols], preferred_element_type=jnp.float32)
            both = jnp.concatenate([got[own, cols], moved.astype(jnp.bfloat16)], axis=0)
            gain[:, cols] += jnp.dot(turned[...], both, preferred_element_type=jnp.float32)
            return 0

        lax.fori_loop(0, tiles, column, 0)
        return 0

    lax.fori_loop(0, groups, gather, 0)

    half = width // 2
    near = tiles // 2

    def push(source, target, send_sem, recv_sem, peer):
        return pltpu.make_async_remote_copy(
            src_ref=source, dst_ref=target, send_sem=send_sem, recv_sem=recv_sem,
            device_id=peer, device_id_type=MESH,
        )

    lend = push(b_ref, b_got, lend_sem.at[0], lend_sem.at[1], partner)

    def columns(k):
        return pl.ds(pl.multiple_of(k * tile, tile), tile)

    def left_part(j):
        return [
            push(
                lent_left.at[j, :, bits], left.at[j, :, bits],
                tile_send.at[i, j], tile_recv.at[i, j], partner,
            )
            for i, bits in enumerate((slice(0, tile), slice(tile, 2 * tile)))
        ]

    def right_part(k):
        return [
            push(
                lent_right.at[i, :, columns(k)], right.at[i, :, columns(k)],
                tile_send.at[i, k], tile_recv.at[i, k], partner,
            )
            for i in range(2)
        ]

    for sub in range(subs):
        b_ref[sub : sub + 1, :] = sigma_gain * moment[:1, sub * LANES : (sub + 1) * LANES]

    def settled(own, cols):
        change = dynamics[own, cols] - sigma_gain * gain[own, cols]
        gain[own, cols] = change
        high = change.astype(jnp.bfloat16)
        return high, (change - high.astype(jnp.float32)).astype(jnp.bfloat16)

    @pl.when(r == 0)
    def _():
        lend.start()

        def settle(k, _):
            cols = columns(k)
            high, low = settled(slice(half, width), cols)
            lent_right[0, :, cols] = high
            lent_right[1, :, cols] = low
            for copy in right_part(k):
                copy.start()
            high, low = settled(slice(0, half), cols)
            right[0, :, cols] = high
            right[1, :, cols] = low
            return 0

        lax.fori_loop(0, tiles, settle, 0)

    @pl.when(r == 1)
    def _():
        def settle_far(j, _):
            for own in (slice(0, half), slice(half, width)):
                high, low = settled(own, columns(j))
                lent_left[j, own, :tile] = high
                lent_left[j, own, tile:] = low
            for copy in left_part(j):
                copy.start()
            return 0

        lax.fori_loop(0, near, settle_far, 0)

        def settle_near(j, _):
            for own in (slice(0, half), slice(half, width)):
                high, low = settled(own, columns(j + near))
                left[j, own, :tile] = high
                left[j, own, tile:] = low
            return 0

        lax.fori_loop(0, near, settle_near, 0)

    lane = lax.broadcasted_iota(jnp.int32, (subs, LANES), 1)
    line = lax.broadcasted_iota(jnp.int32, (subs, LANES), 0)
    group = 16

    def apply(matrix, vector):
        pieces = [jnp.broadcast_to(vector[k : k + 1, :], (subs, LANES)) for k in range(subs)]

        def rows(step, total):
            for inner in range(group):
                g = step * group + inner
                own = pl.ds(pl.multiple_of(g * subs, subs), subs)
                part = matrix[own, 0:LANES] * pieces[0]
                for k in range(1, subs):
                    part = part + matrix[own, k * LANES : (k + 1) * LANES] * pieces[k]
                total = jnp.where(lane == g, jnp.sum(part, axis=1, keepdims=True), total)
            return total

        total = lax.fori_loop(0, LANES // group, rows, jnp.zeros((subs, LANES), jnp.float32))
        result = jnp.zeros((subs, LANES), jnp.float32)
        for k in range(subs):
            spots = lane // subs + k * (LANES // subs)
            moved = jnp.take_along_axis(total, spots, axis=1)
            kept = jnp.where(line == lax.rem(lane, subs), moved, 0.0)
            result = jnp.where(line == k, jnp.sum(kept, axis=0, keepdims=True), result)
        return result

    def product(j, cols):
        own = pl.ds(pl.multiple_of(j * tile, tile), tile)
        high, low = right[0, own, cols], right[1, own, cols]
        return jnp.dot(
            left[j], jnp.concatenate([high, high], axis=0), preferred_element_type=jnp.float32
        ) + jnp.dot(left[j, :, :tile], low, preferred_element_type=jnp.float32)

    @pl.when(r == 0)
    def _():
        def compose(j, _):
            for copy in left_part(j):
                copy.wait_recv()

            def fill(k, _):
                cols = columns(k)

                @pl.when(j == 0)
                def _():
                    whole[:, cols] = gain[:, cols] + product(j, cols)

                @pl.when(j > 0)
                def _():
                    whole[:, cols] += product(j, cols)

                return 0

            lax.fori_loop(0, tiles, fill, 0)
            return 0

        lax.fori_loop(0, near, compose, 0)
        lend.wait_send()

        def drain(k, _):
            for copy in right_part(k):
                copy.wait_send()
            return 0

        lax.fori_loop(0, tiles, drain, 0)

    @pl.when(r == 1)
    def _():
        lend.wait_recv()
        b_ref[...] += apply(gain, b_got[...])

        def compose(k, _):
            for copy in right_part(k):
                copy.wait_recv()
            cols = columns(k)
            total = gain[:, cols] + product(0, cols)
            for j in range(1, near):
                total = total + product(j, cols)
            whole[:, cols] = total
            return 0

        lax.fori_loop(0, tiles, compose, 0)

        def drain(j, _):
            for copy in left_part(j):
                copy.wait_send()
            return 0

        lax.fori_loop(0, near, drain, 0)

    def onward(core, sender):
        return push(
            went, came.at[sender], pass_send.at[core], pass_recv.at[sender], (after, core)
        )

    @pl.when(place_here == 0)
    def _():
        came[0] = start_ref[...]
        came[1] = jnp.zeros_like(start_ref)

    @pl.when(place_here > 0)
    def _():
        for core in range(2):
            onward(core, core).wait_recv()

    state = came[0] + came[1]
    share_of = jnp.where(r == 0, 1.0, 0.0)
    went[...] = apply(whole, state) + (b_ref[...] + share_of * state)
    passing = place_here < last

    @pl.when(passing)
    def _():
        for core in range(2):
            onward(core, r).start()

    stays = place_here == t

    def report(source, core, slot):
        return push(
            source, back.at[slot], out_send.at[slot, core], out_recv.at[slot], (place_here, core)
        )

    def tell(source, slot):
        for core in range(2):
            @pl.when(jnp.logical_not(stays & (r == core)))
            def _():
                report(source, core, slot).start()

            @pl.when(stays & (r == core))
            def _():
                back[slot] = source[...]

    @pl.when(r == 0)
    def _():
        tell(went, 1)
        middle[...] = apply(gain, state) + (b_ref[...] + state)
        tell(middle, 0)

    @pl.when(r == 1)
    def _():
        tell(went, 2)

    for slot, sender in ((1, 0), (2, 1), (0, 0)):
        @pl.when(jnp.logical_not(stays & (r == sender)))
        def _():
            report(went, r, slot).wait_recv()

    for core in range(2):
        @pl.when(jnp.logical_not(stays & (r == core)))
        def _():
            @pl.when(r == 0)
            def _():
                report(went, core, 1).wait_send()
                report(middle, core, 0).wait_send()

            @pl.when(r == 1)
            def _():
                report(went, core, 2).wait_send()

    part = subs // 2

    @pl.when(r == 0)
    def _():
        out_ref[0] = back[0, :part, :]
        out_ref[1] = back[1, :part, :] + back[2, :part, :]

    @pl.when(r == 1)
    def _():
        out_ref[0] = back[0, part:, :]
        out_ref[1] = back[1, part:, :] + back[2, part:, :]

    @pl.when(passing)
    def _():
        for core in range(2):
            onward(core, r).wait_send()

    def finish(slab, _):
        @pl.when(slab != me)
        def _():
            rows, tags = copies(slab, here)
            rows.wait_send()

            @pl.when(r == 0)
            def _():
                tags.wait_send()

        return 0

    lax.fori_loop(0, slabs, finish, 0)


def body(initial, dynamics, obs_rows, obs_values, obs_slab):
    time_devs = lax.axis_size("tm")
    row_devs = lax.axis_size("row")
    width = dynamics.shape[1]
    count, local = obs_rows.shape
    slabs = time_devs * row_devs
    subs = width // LANES
    tiles = width // 256
    vmem = pl.BlockSpec(memory_space=pltpu.VMEM)
    anywhere = pl.BlockSpec(memory_space=pl.ANY)
    small = pltpu.VMEM((subs, LANES), jnp.float32)
    square = pltpu.VMEM((width, width), jnp.float32)
    columns = pltpu.VMEM((tiles // 2, width, 512), jnp.bfloat16)
    lines = pltpu.VMEM((2, width // 2, width), jnp.bfloat16)
    sems = pltpu.SemaphoreType.DMA((slabs,))
    states = pl.pallas_call(
        observer_kernel,
        out_shape=jax.ShapeDtypeStruct((2, subs // 2, LANES), jnp.float32),
        in_specs=[vmem, anywhere, vmem, anywhere, vmem],
        out_specs=vmem,
        scratch_shapes=[
            pltpu.VMEM((count, local), jnp.bfloat16),
            pltpu.VMEM((1, count), jnp.float32),
            pltpu.VMEM((slabs, CAP, local), jnp.bfloat16),
            pltpu.VMEM((slabs, 1, LANES), jnp.float32),
            pltpu.VMEM((1, count), jnp.int32),
            pltpu.VMEM((time_devs * CAP, width), jnp.bfloat16),
            pltpu.VMEM((slabs, 1, LANES), jnp.float32),
            square,
            pltpu.VMEM((width, width), jnp.bfloat16),
            pltpu.VMEM((width, 512), jnp.bfloat16),
            square,
            pltpu.VMEM((8, width), jnp.float32),
            square,
            columns,
            columns,
            lines,
            lines,
            small,
            small,
            pltpu.VMEM((2, subs, LANES), jnp.float32),
            small,
            small,
            pltpu.VMEM((3, subs, LANES), jnp.float32),
            sems,
            sems,
            sems,
            sems,
            pltpu.SemaphoreType.DMA((4,)),
            pltpu.SemaphoreType.DMA((2,)),
            pltpu.SemaphoreType.DMA((2, tiles)),
            pltpu.SemaphoreType.DMA((2, tiles)),
            pltpu.SemaphoreType.DMA((2,)),
            pltpu.SemaphoreType.DMA((2,)),
            pltpu.SemaphoreType.DMA((3, 2)),
            pltpu.SemaphoreType.DMA((3,)),
        ],
        compiler_params=pltpu.CompilerParams(
            collective_id=0, has_side_effects=True, vmem_limit_bytes=60 << 20
        ),
        name="observer",
    )(
        obs_slab.reshape(1, -1),
        obs_rows,
        obs_values.reshape(-1, LANES),
        dynamics,
        initial.reshape(subs, LANES),
    )
    return states.reshape(2, width // 2)


def solution(mesh):
    placed = (P(), P(), P("tm", "row"), P("tm"), P("tm", None))
    return jax.shard_map(
        body, mesh=mesh, in_specs=placed, out_specs=P("tm", "row"), check_vma=False
    )
```

time: 111 us -> 110 us (level); the launches traced: 111 us -> 108 us
  local copies, waits for them, and re-layouts: 2.55 us -> 1.28 us
    reshape x1 -> x0, local copies, waits for them, and re-layouts: 1.29 us -> none  [body(): obs_values.reshape(1, -1)]
    pallas_call x1, Pallas kernels: 108 us -> 107 us  [body(): pl.pallas_call(observer_kernel, out_shape=jax.ShapeDtypeStruct((2, subs /...]
where the time goes in v2:
time: 110 us; the launch traced here: 108 us
  Pallas kernels  107 us (97%)
  local copies, waits for them, and re-layouts  1.28 us (1%)
    pallas_call x1, Pallas kernels, body(): pl.pallas_call(observer_kernel, out_shape=jax.ShapeDtypeStruct((2, subs /...  107 us

profile of v2, /device:TPU:29, one launch (start us, length us, event | category | flops | bytes accessed | tf_op | source)
XLA Modules:
  0.0 108.2 jit_solution(5645768921752066094)
XLA Ops:
  0.0 107.0 %observer.1 = f32[2,4,128]{2,1,0:T(4,128)} custom-call(s32[1,2048]{1,0:T(1,128)} %bitcast.8, bf16[2048,512]{1,0:T(8,128)(2,1)} %rows_hbm.1, bf16[16,128]{1,0:T(8,128)(2,1)} %bitcast.9, f32[1024,1024]{1,0:T(8,128)} %dynamics_ref.1, f32[8,128]{1,0:T(8,128)} %bitcast.10), custom_call_target="tpu_custom_call" | custom-call | tf_op jit(solution)/shard_map/observer/pallas_call | solution.py:521
  107.0 1.3 %copy.8 = f32[1,2,4,128]{3,1,2,0:T(2,128)} copy(f32[1,2,4,128]{3,2,1,0:T(4,128)} %bitcast.7) | data formatting | bytes 8192

commit v3 on v2

--- a/solution.py
+++ b/solution.py
@@ -36,7 +36,7 @@
 def observer_kernel(
     target_ref, rows_hbm, values_ref, dynamics_ref, start_ref, out_ref,
     rows_ref, values_row, sent, sent_values, slot_ref, got, got_values, dynamics, dyn_high, turned, gain, moment,
-    whole, left, lent_left, right, lent_right, b_ref, b_got, came, went, middle, back,
+    whole, halves, right, b_ref, b_got, came, went, back,
     row_send, row_recv, value_send, value_recv, own_sem, lend_sem, tile_send, tile_recv, pass_send, pass_recv,
     out_send, out_recv,
 ):
@@ -232,9 +232,6 @@
 
     lax.fori_loop(0, groups, gather, 0)
 
-    half = width // 2
-    near = tiles // 2
-
     def push(source, target, send_sem, recv_sem, peer):
         return pltpu.make_async_remote_copy(
             src_ref=source, dst_ref=target, send_sem=send_sem, recv_sem=recv_sem,
@@ -246,19 +243,10 @@
     def columns(k):
         return pl.ds(pl.multiple_of(k * tile, tile), tile)
 
-    def left_part(j):
+    def part(k):
         return [
             push(
-                lent_left.at[j, :, bits], left.at[j, :, bits],
-                tile_send.at[i, j], tile_recv.at[i, j], partner,
-            )
-            for i, bits in enumerate((slice(0, tile), slice(tile, 2 * tile)))
-        ]
-
-    def right_part(k):
-        return [
-            push(
-                lent_right.at[i, :, columns(k)], right.at[i, :, columns(k)],
+                halves.at[i, :, columns(k)], right.at[i, :, columns(k)],
                 tile_send.at[i, k], tile_recv.at[i, k], partner,
             )
             for i in range(2)
@@ -267,55 +255,30 @@
     for sub in range(subs):
         b_ref[sub : sub + 1, :] = sigma_gain * moment[:1, sub * LANES : (sub + 1) * LANES]
 
-    def settled(own, cols):
-        change = dynamics[own, cols] - sigma_gain * gain[own, cols]
-        gain[own, cols] = change
+    @pl.when(r == 0)
+    def _():
+        lend.start()
+
+    def settle(k, _):
+        cols = columns(k)
+        change = dynamics[:, cols] - sigma_gain * gain[:, cols]
+        gain[:, cols] = change
         high = change.astype(jnp.bfloat16)
-        return high, (change - high.astype(jnp.float32)).astype(jnp.bfloat16)
-
-    @pl.when(r == 0)
-    def _():
-        lend.start()
-
-        def settle(k, _):
-            cols = columns(k)
-            high, low = settled(slice(half, width), cols)
-            lent_right[0, :, cols] = high
-            lent_right[1, :, cols] = low
-            for copy in right_part(k):
+        halves[0, :, cols] = high
+        halves[1, :, cols] = (change - high.astype(jnp.float32)).astype(jnp.bfloat16)
+
+        @pl.when(r == 0)
+        def _():
+            for copy in part(k):
                 copy.start()
-            high, low = settled(slice(0, half), cols)
-            right[0, :, cols] = high
-            right[1, :, cols] = low
-            return 0
-
-        lax.fori_loop(0, tiles, settle, 0)
-
-    @pl.when(r == 1)
-    def _():
-        def settle_far(j, _):
-            for own in (slice(0, half), slice(half, width)):
-                high, low = settled(own, columns(j))
-                lent_left[j, own, :tile] = high
-                lent_left[j, own, tile:] = low
-            for copy in left_part(j):
-                copy.start()
-            return 0
-
-        lax.fori_loop(0, near, settle_far, 0)
-
-        def settle_near(j, _):
-            for own in (slice(0, half), slice(half, width)):
-                high, low = settled(own, columns(j + near))
-                left[j, own, :tile] = high
-                left[j, own, tile:] = low
-            return 0
-
-        lax.fori_loop(0, near, settle_near, 0)
+
+        return 0
+
+    lax.fori_loop(0, tiles, settle, 0)
 
     lane = lax.broadcasted_iota(jnp.int32, (subs, LANES), 1)
     line = lax.broadcasted_iota(jnp.int32, (subs, LANES), 0)
-    group = 16
+    group = 64
 
     def apply(matrix, vector):
         pieces = [jnp.broadcast_to(vector[k : k + 1, :], (subs, LANES)) for k in range(subs)]
@@ -339,40 +302,12 @@
             result = jnp.where(line == k, jnp.sum(kept, axis=0, keepdims=True), result)
         return result
 
-    def product(j, cols):
-        own = pl.ds(pl.multiple_of(j * tile, tile), tile)
-        high, low = right[0, own, cols], right[1, own, cols]
-        return jnp.dot(
-            left[j], jnp.concatenate([high, high], axis=0), preferred_element_type=jnp.float32
-        ) + jnp.dot(left[j, :, :tile], low, preferred_element_type=jnp.float32)
-
     @pl.when(r == 0)
     def _():
-        def compose(j, _):
-            for copy in left_part(j):
-                copy.wait_recv()
-
-            def fill(k, _):
-                cols = columns(k)
-
-                @pl.when(j == 0)
-                def _():
-                    whole[:, cols] = gain[:, cols] + product(j, cols)
-
-                @pl.when(j > 0)
-                def _():
-                    whole[:, cols] += product(j, cols)
-
-                return 0
-
-            lax.fori_loop(0, tiles, fill, 0)
-            return 0
-
-        lax.fori_loop(0, near, compose, 0)
         lend.wait_send()
 
         def drain(k, _):
-            for copy in right_part(k):
+            for copy in part(k):
                 copy.wait_send()
             return 0
 
@@ -381,112 +316,89 @@
     @pl.when(r == 1)
     def _():
         lend.wait_recv()
-        b_ref[...] += apply(gain, b_got[...])
+        b_ref[...] += b_got[...] + apply(gain, b_got[...])
 
         def compose(k, _):
-            for copy in right_part(k):
+            for copy in part(k):
                 copy.wait_recv()
             cols = columns(k)
-            total = gain[:, cols] + product(0, cols)
-            for j in range(1, near):
-                total = total + product(j, cols)
-            whole[:, cols] = total
+            high, low = right[0, :, cols], right[1, :, cols]
+            whole[:, cols] = (
+                gain[:, cols] + (high.astype(jnp.float32) + low.astype(jnp.float32))
+                + jnp.dot(halves[0], high, preferred_element_type=jnp.float32)
+                + jnp.dot(halves[0], low, preferred_element_type=jnp.float32)
+                + jnp.dot(halves[1], high, preferred_element_type=jnp.float32)
+            )
             return 0
 
         lax.fori_loop(0, tiles, compose, 0)
 
-        def drain(j, _):
-            for copy in left_part(j):
-                copy.wait_send()
-            return 0
-
-        lax.fori_loop(0, near, drain, 0)
-
-    def onward(core, sender):
+    onward = push(went, came, pass_send.at[1], pass_recv.at[0], (after, 1))
+    aside = push(went, came, pass_send.at[0], pass_recv.at[0], (after, 0))
+
+    @pl.when(place_here == 0)
+    def _():
+        came[...] = start_ref[...]
+
+    @pl.when(place_here > 0)
+    def _():
+        onward.wait_recv()
+
+    passing = (r == 1) & (place_here < last)
+
+    @pl.when(r == 1)
+    def _():
+        state = came[...]
+        went[...] = apply(whole, state) + (b_ref[...] + state)
+
+    @pl.when(passing)
+    def _():
+        onward.start()
+        aside.start()
+
+    @pl.when(r == 0)
+    def _():
+        state = came[...]
+        went[...] = apply(gain, state) + (b_ref[...] + state)
+
+    stays = place_here == t
+
+    def report(core, sender):
         return push(
-            went, came.at[sender], pass_send.at[core], pass_recv.at[sender], (after, core)
+            went, back.at[sender], out_send.at[core], out_recv.at[sender], (place_here, core)
         )
-
-    @pl.when(place_here == 0)
-    def _():
-        came[0] = start_ref[...]
-        came[1] = jnp.zeros_like(start_ref)
-
-    @pl.when(place_here > 0)
-    def _():
-        for core in range(2):
-            onward(core, core).wait_recv()
-
-    state = came[0] + came[1]
-    share_of = jnp.where(r == 0, 1.0, 0.0)
-    went[...] = apply(whole, state) + (b_ref[...] + share_of * state)
-    passing = place_here < last
-
-    @pl.when(passing)
-    def _():
-        for core in range(2):
-            onward(core, r).start()
-
-    stays = place_here == t
-
-    def report(source, core, slot):
-        return push(
-            source, back.at[slot], out_send.at[slot, core], out_recv.at[slot], (place_here, core)
-        )
-
-    def tell(source, slot):
-        for core in range(2):
-            @pl.when(jnp.logical_not(stays & (r == core)))
-            def _():
-                report(source, core, slot).start()
-
-            @pl.when(stays & (r == core))
-            def _():
-                back[slot] = source[...]
-
-    @pl.when(r == 0)
-    def _():
-        tell(went, 1)
-        middle[...] = apply(gain, state) + (b_ref[...] + state)
-        tell(middle, 0)
-
-    @pl.when(r == 1)
-    def _():
-        tell(went, 2)
-
-    for slot, sender in ((1, 0), (2, 1), (0, 0)):
-        @pl.when(jnp.logical_not(stays & (r == sender)))
-        def _():
-            report(went, r, slot).wait_recv()
 
     for core in range(2):
         @pl.when(jnp.logical_not(stays & (r == core)))
         def _():
-            @pl.when(r == 0)
-            def _():
-                report(went, core, 1).wait_send()
-                report(middle, core, 0).wait_send()
-
-            @pl.when(r == 1)
-            def _():
-                report(went, core, 2).wait_send()
+            report(core, r).start()
+
+        @pl.when(stays & (r == core))
+        def _():
+            back[core] = went[...]
+
+    for core in range(2):
+        @pl.when(jnp.logical_not(stays & (r == core)))
+        def _():
+            report(core, core).wait_recv()
+            report(core, r).wait_send()
 
     part = subs // 2
 
     @pl.when(r == 0)
     def _():
         out_ref[0] = back[0, :part, :]
-        out_ref[1] = back[1, :part, :] + back[2, :part, :]
+        out_ref[1] = back[1, :part, :]
 
     @pl.when(r == 1)
     def _():
         out_ref[0] = back[0, part:, :]
-        out_ref[1] = back[1, part:, :] + back[2, part:, :]
+        out_ref[1] = back[1, part:, :]
 
     @pl.when(passing)
     def _():
-        for core in range(2):
-            onward(core, r).wait_send()
+        onward.wait_send()
+        aside.wait_send()
 
     def finish(slab, _):
         @pl.when(slab != me)
@@ -515,8 +427,7 @@
     anywhere = pl.BlockSpec(memory_space=pl.ANY)
     small = pltpu.VMEM((subs, LANES), jnp.float32)
     square = pltpu.VMEM((width, width), jnp.float32)
-    columns = pltpu.VMEM((tiles // 2, width, 512), jnp.bfloat16)
-    lines = pltpu.VMEM((2, width // 2, width), jnp.bfloat16)
+    halves = pltpu.VMEM((2, width, width), jnp.bfloat16)
     sems = pltpu.SemaphoreType.DMA((slabs,))
     states = pl.pallas_call(
         observer_kernel,
@@ -537,16 +448,13 @@
             square,
             pltpu.VMEM((8, width), jnp.float32),
             square,
-            columns,
-            columns,
-            lines,
-            lines,
+            halves,
+            halves,
+            small,
+            small,
             small,
             small,
             pltpu.VMEM((2, subs, LANES), jnp.float32),
-            small,
-            small,
-            pltpu.VMEM((3, subs, LANES), jnp.float32),
             sems,
             sems,
             sems,
@@ -556,9 +464,9 @@
             pltpu.SemaphoreType.DMA((2, tiles)),
             pltpu.SemaphoreType.DMA((2, tiles)),
             pltpu.SemaphoreType.DMA((2,)),
+            pltpu.SemaphoreType.DMA((1,)),
             pltpu.SemaphoreType.DMA((2,)),
-            pltpu.SemaphoreType.DMA((3, 2)),
-            pltpu.SemaphoreType.DMA((3,)),
+            pltpu.SemaphoreType.DMA((2,)),
         ],
         compiler_params=pltpu.CompilerParams(
             collective_id=0, has_side_effects=True, vmem_limit_bytes=60 << 20

time: 110 us -> 90.5 us (0.82); the launches traced: 108 us -> 90.3 us
  Pallas kernels: 107 us -> 89 us
    pallas_call x1, Pallas kernels: 107 us -> 89 us  [body(): pl.pallas_call(observer_kernel, out_shape=jax.ShapeDtypeStruct((2, subs /...]
where the time goes in v3:
time: 90.5 us; the launch traced here: 90.3 us
  Pallas kernels  89 us (98%)
  local copies, waits for them, and re-layouts  1.28 us (1%)
    pallas_call x1, Pallas kernels, body(): pl.pallas_call(observer_kernel, out_shape=jax.ShapeDtypeStruct((2, subs /...  89 us

profile of v3, /device:TPU:29, one launch (start us, length us, event | category | flops | bytes accessed | tf_op | source)
XLA Modules:
  0.0 90.3 jit_solution(7068014270075354382)
XLA Ops:
  0.0 89.0 %observer.1 = f32[2,4,128]{2,1,0:T(4,128)} custom-call(s32[1,2048]{1,0:T(1,128)} %bitcast.8, bf16[2048,512]{1,0:T(8,128)(2,1)} %rows_hbm.1, bf16[16,128]{1,0:T(8,128)(2,1)} %bitcast.9, f32[1024,1024]{1,0:T(8,128)} %dynamics_ref.1, f32[8,128]{1,0:T(8,128)} %bitcast.10), custom_call_target="tpu_custom_call" | custom-call | tf_op jit(solution)/shard_map/observer/pallas_call | solution.py:432
  89.0 1.3 %copy.8 = f32[1,2,4,128]{3,1,2,0:T(2,128)} copy(f32[1,2,4,128]{3,2,1,0:T(4,128)} %bitcast.7) | data formatting | bytes 8192

commit v4 on v3

--- a/solution.py
+++ b/solution.py
@@ -35,7 +35,7 @@
 
 def observer_kernel(
     target_ref, rows_hbm, values_ref, dynamics_ref, start_ref, out_ref,
-    rows_ref, values_row, sent, sent_values, slot_ref, got, got_values, dynamics, dyn_high, turned, gain, moment,
+    rows_ref, values_row, sent, sent_values, slot_ref, got, got_values, dynamics, dyn_high, turned, rounded, gain, moment,
     whole, halves, right, b_ref, b_got, came, went, back,
     row_send, row_recv, value_send, value_recv, own_sem, lend_sem, tile_send, tile_recv, pass_send, pass_recv,
     out_send, out_recv,
@@ -55,6 +55,7 @@
     subs = width // LANES
     tile = 256
     tiles = width // tile
+    wide = 2 * tile
     block = 256
     share = block // CAP
     blocks = slabs // share
@@ -211,9 +212,7 @@
         lax.fori_loop(at * chips * row_devs, (at + 1) * chips * row_devs, arrive, 0)
         own = pl.ds(pl.multiple_of(at * block, block), block)
         rows = got[own, :]
-        flipped = rows.T
-        turned[:, :block] = flipped
-        turned[:, block:] = flipped
+        turned[...] = rows.T
         tags = jnp.concatenate(
             [got_values[(at * chips + k) * row_devs][:, :CAP] for k in range(chips)], axis=1
         )
@@ -221,13 +220,11 @@
         moment[...] += jnp.dot(tags, rows, preferred_element_type=jnp.float32)
 
         def column(k, _):
-            cols = pl.ds(pl.multiple_of(k * tile, tile), tile)
-            moved = jnp.dot(got[own, :], dyn_high[:, cols], preferred_element_type=jnp.float32)
-            both = jnp.concatenate([got[own, cols], moved.astype(jnp.bfloat16)], axis=0)
-            gain[:, cols] += jnp.dot(turned[...], both, preferred_element_type=jnp.float32)
+            cols = pl.ds(pl.multiple_of(k * wide, wide), wide)
+            gain[:, cols] += jnp.dot(turned[...], got[own, cols], preferred_element_type=jnp.float32)
             return 0
 
-        lax.fori_loop(0, tiles, column, 0)
+        lax.fori_loop(0, width // wide, column, 0)
         return 0
 
     lax.fori_loop(0, groups, gather, 0)
@@ -243,42 +240,54 @@
     def columns(k):
         return pl.ds(pl.multiple_of(k * tile, tile), tile)
 
-    def part(k):
-        return [
-            push(
-                halves.at[i, :, columns(k)], right.at[i, :, columns(k)],
-                tile_send.at[i, k], tile_recv.at[i, k], partner,
-            )
-            for i in range(2)
-        ]
+    def part(i, k):
+        cols = columns(k)
+        return push(
+            halves.at[i, :, cols], right.at[i, :, cols], tile_send.at[i, k], tile_recv.at[i, k], partner,
+        )
 
     for sub in range(subs):
         b_ref[sub : sub + 1, :] = sigma_gain * moment[:1, sub * LANES : (sub + 1) * LANES]
 
-    @pl.when(r == 0)
-    def _():
-        lend.start()
-
-    def settle(k, _):
-        cols = columns(k)
-        change = dynamics[:, cols] - sigma_gain * gain[:, cols]
+    for k in range(tiles):
+        rows = slice(k * tile, (k + 1) * tile)
+        rounded[rows, :] = gain[rows, :].astype(jnp.bfloat16)
+
+    def span(k):
+        return pl.ds(pl.multiple_of(k * wide, wide), wide)
+
+    def settle(cols):
+        moved = jnp.dot(rounded[...], dyn_high[:, cols], preferred_element_type=jnp.float32)
+        change = dynamics[:, cols] - sigma_gain * (gain[:, cols] + moved)
         gain[:, cols] = change
         high = change.astype(jnp.bfloat16)
         halves[0, :, cols] = high
         halves[1, :, cols] = (change - high.astype(jnp.float32)).astype(jnp.bfloat16)
 
-        @pl.when(r == 0)
-        def _():
-            for copy in part(k):
-                copy.start()
-
-        return 0
-
-    lax.fori_loop(0, tiles, settle, 0)
+    @pl.when(r == 0)
+    def _():
+        lend.start()
+
+        def settle_sent(k, _):
+            settle(columns(k))
+            part(0, k).start()
+            return 0
+
+        lax.fori_loop(0, tiles, settle_sent, 0)
+        for k in range(tiles):
+            part(1, k).start()
+
+    @pl.when(r == 1)
+    def _():
+        def settle_kept(k, _):
+            settle(span(k))
+            return 0
+
+        lax.fori_loop(0, width // wide, settle_kept, 0)
 
     lane = lax.broadcasted_iota(jnp.int32, (subs, LANES), 1)
     line = lax.broadcasted_iota(jnp.int32, (subs, LANES), 0)
-    group = 64
+    group = LANES
 
     def apply(matrix, vector):
         pieces = [jnp.broadcast_to(vector[k : k + 1, :], (subs, LANES)) for k in range(subs)]
@@ -305,33 +314,39 @@
     @pl.when(r == 0)
     def _():
         lend.wait_send()
-
-        def drain(k, _):
-            for copy in part(k):
-                copy.wait_send()
-            return 0
-
-        lax.fori_loop(0, tiles, drain, 0)
+        for i in range(2):
+            for k in range(tiles):
+                part(i, k).wait_send()
 
     @pl.when(r == 1)
     def _():
         lend.wait_recv()
         b_ref[...] += b_got[...] + apply(gain, b_got[...])
-
-        def compose(k, _):
-            for copy in part(k):
-                copy.wait_recv()
-            cols = columns(k)
-            high, low = right[0, :, cols], right[1, :, cols]
+        def compose_high(k, _):
+            for inner in range(wide // tile):
+                part(0, k * (wide // tile) + inner).wait_recv()
+            cols = span(k)
+            high = right[0, :, cols]
             whole[:, cols] = (
-                gain[:, cols] + (high.astype(jnp.float32) + low.astype(jnp.float32))
+                gain[:, cols] + high.astype(jnp.float32)
                 + jnp.dot(halves[0], high, preferred_element_type=jnp.float32)
-                + jnp.dot(halves[0], low, preferred_element_type=jnp.float32)
                 + jnp.dot(halves[1], high, preferred_element_type=jnp.float32)
             )
             return 0
 
-        lax.fori_loop(0, tiles, compose, 0)
+        lax.fori_loop(0, width // wide, compose_high, 0)
+
+        def compose_low(k, _):
+            for inner in range(wide // tile):
+                part(1, k * (wide // tile) + inner).wait_recv()
+            cols = span(k)
+            low = right[1, :, cols]
+            whole[:, cols] += low.astype(jnp.float32) + jnp.dot(
+                halves[0], low, preferred_element_type=jnp.float32
+            )
+            return 0
+
+        lax.fori_loop(0, width // wide, compose_low, 0)
 
     onward = push(went, came, pass_send.at[1], pass_recv.at[0], (after, 1))
     aside = push(went, came, pass_send.at[0], pass_recv.at[0], (after, 0))
@@ -444,7 +459,8 @@
             pltpu.VMEM((slabs, 1, LANES), jnp.float32),
             square,
             pltpu.VMEM((width, width), jnp.bfloat16),
-            pltpu.VMEM((width, 512), jnp.bfloat16),
+            pltpu.VMEM((width, 256), jnp.bfloat16),
+            pltpu.VMEM((width, width), jnp.bfloat16),
             square,
             pltpu.VMEM((8, width), jnp.float32),
             square,

time: 90.5 us -> 85.1 us (0.940)
  Pallas kernels: 89 us -> 83.6 us
    pallas_call x1, Pallas kernels: 89 us -> 83.6 us  [body(): pl.pallas_call(observer_kernel, out_shape=jax.ShapeDtypeStruct((2, subs /...]
where the time goes in v4:
time: 85.1 us; the launch traced here: 84.9 us
  Pallas kernels  83.6 us (98%)
  local copies, waits for them, and re-layouts  1.28 us (2%)
    pallas_call x1, Pallas kernels, body(): pl.pallas_call(observer_kernel, out_shape=jax.ShapeDtypeStruct((2, subs /...  83.6 us

profile of v4, /device:TPU:29, one launch (start us, length us, event | category | flops | bytes accessed | tf_op | source)
XLA Modules:
  0.0 84.9 jit_solution(15011006337467270120)
XLA Ops:
  0.0 83.6 %observer.1 = f32[2,4,128]{2,1,0:T(4,128)} custom-call(s32[1,2048]{1,0:T(1,128)} %bitcast.8, bf16[2048,512]{1,0:T(8,128)(2,1)} %rows_hbm.1, bf16[16,128]{1,0:T(8,128)(2,1)} %bitcast.9, f32[1024,1024]{1,0:T(8,128)} %dynamics_ref.1, f32[8,128]{1,0:T(8,128)} %bitcast.10), custom_call_target="tpu_custom_call" | custom-call | tf_op jit(solution)/shard_map/observer/pallas_call | solution.py:447
  83.6 1.3 %copy.8 = f32[1,2,4,128]{3,1,2,0:T(2,128)} copy(f32[1,2,4,128]{3,2,1,0:T(4,128)} %bitcast.7) | data formatting | bytes 8192

commit v5 on v4

--- a/solution.py
+++ b/solution.py
@@ -37,7 +37,7 @@
     target_ref, rows_hbm, values_ref, dynamics_ref, start_ref, out_ref,
     rows_ref, values_row, sent, sent_values, slot_ref, got, got_values, dynamics, dyn_high, turned, rounded, gain, moment,
     whole, halves, right, b_ref, b_got, came, went, back,
-    row_send, row_recv, value_send, value_recv, own_sem, lend_sem, tile_send, tile_recv, pass_send, pass_recv,
+    all_sent, row_recv, value_recv, own_sem, lend_sem, tile_send, tile_recv, pass_send, pass_recv,
     out_send, out_recv,
 ):
     time_devs, row_devs = lax.axis_size("tm"), lax.axis_size("row")
@@ -65,17 +65,18 @@
 
     barrier = pltpu.get_barrier_semaphore()
 
-    def greet(slab, _):
-        @pl.when(slab != me)
-        def _():
-            pl.semaphore_signal(barrier, inc=1, device_id=device(slab), device_id_type=MESH)
-
+    def greet(turn, _):
+        other = visit(here, slabs - 1 - turn, slabs)
+        pl.semaphore_signal(
+            barrier, inc=1, device_id=(other // row_devs, lax.rem(other, row_devs)),
+            device_id_type=MESH,
+        )
         return 0
 
-    lax.fori_loop(0, slabs, greet, 0)
-    rows_in = pltpu.make_async_copy(rows_hbm, rows_ref, own_sem.at[3])
+    lax.fori_loop(0, slabs - 1, greet, 0)
+    rows_in = pltpu.make_async_copy(rows_hbm, rows_ref, own_sem.at[1])
     rows_in.start()
-    fetch = pltpu.make_async_copy(dynamics_ref, dynamics, own_sem.at[2])
+    fetch = pltpu.make_async_copy(dynamics_ref, dynamics, own_sem.at[0])
     fetch.start()
 
     before = (
@@ -102,22 +103,26 @@
         cols = pl.ds(pl.multiple_of(lax.rem(source, row_devs) * local, local), local)
         return got.at[rows, cols]
 
-    def copies(slab, source):
+    chips = block // CAP
+    groups = time_devs // chips
+    nearest = t // chips
+
+    def copies(slab):
         rows = pltpu.make_async_remote_copy(
-            src_ref=sent.at[slab], dst_ref=landing(source),
-            send_sem=row_send.at[slab], recv_sem=row_recv.at[source],
+            src_ref=sent.at[slab], dst_ref=landing(here),
+            send_sem=all_sent.at[0], recv_sem=row_recv.at[nearest],
             device_id=device(slab), device_id_type=MESH,
         )
         tags = pltpu.make_async_remote_copy(
-            src_ref=sent_values.at[slab], dst_ref=got_values.at[source],
-            send_sem=value_send.at[slab], recv_sem=value_recv.at[source],
+            src_ref=sent_values.at[slab], dst_ref=got_values.at[t],
+            send_sem=all_sent.at[1], recv_sem=value_recv.at[nearest],
             device_id=device(slab), device_id_type=MESH,
         )
         return rows, tags
 
     keep = (
-        pltpu.make_async_copy(sent.at[me], landing(here), own_sem.at[0]),
-        pltpu.make_async_copy(sent_values.at[me], got_values.at[here], own_sem.at[1]),
+        pltpu.make_async_copy(sent.at[me], landing(here), row_recv.at[nearest]),
+        pltpu.make_async_copy(sent_values.at[me], got_values.at[t], value_recv.at[nearest]),
     )
 
     def place(at):
@@ -136,6 +141,8 @@
     depth = t // 4
 
     def order(turn):
+        mixed = lax.rem(turn, 2) * column_blocks + turn // 2
+        turn = jnp.where(((t >> 1) & 1 == 0) & (turn < 2 * column_blocks), mixed, turn)
         column = turn // column_blocks
         along = jnp.where(column & 1 == 1, depth, planes - 1 - depth)
         own = along * row_devs // share
@@ -149,7 +156,7 @@
 
             @pl.when(slab != me)
             def _():
-                rows, tags = copies(slab, here)
+                rows, tags = copies(slab)
                 rows.start()
 
                 @pl.when(r == 0)
@@ -158,8 +165,11 @@
 
             @pl.when(slab == me)
             def _():
-                for copy in keep:
-                    copy.start()
+                keep[0].start()
+
+                @pl.when(r == 0)
+                def _():
+                    keep[1].start()
 
     rows_in.wait()
     place(order(0)[0])
@@ -185,36 +195,16 @@
     gain[...] = jnp.zeros_like(gain)
     moment[...] = jnp.zeros_like(moment)
 
-    chips = block // CAP
-    groups = time_devs // chips
-    nearest = t // chips
-
     def gather(turn, _):
         at = visit(nearest, turn, groups)
-
-        def arrive(source, _):
-            @pl.when(source != here)
-            def _():
-                rows, tags = copies(me, source)
-                rows.wait_recv()
-
-                @pl.when(lax.rem(source, row_devs) == 0)
-                def _():
-                    tags.wait_recv()
-
-            @pl.when(source == here)
-            def _():
-                for copy in keep:
-                    copy.wait()
-
-            return 0
-
-        lax.fori_loop(at * chips * row_devs, (at + 1) * chips * row_devs, arrive, 0)
         own = pl.ds(pl.multiple_of(at * block, block), block)
+        named = pl.ds(at * chips, chips)
+        pltpu.make_async_copy(got.at[own], got.at[own], row_recv.at[at]).wait()
+        pltpu.make_async_copy(got_values.at[named], got_values.at[named], value_recv.at[at]).wait()
         rows = got[own, :]
         turned[...] = rows.T
         tags = jnp.concatenate(
-            [got_values[(at * chips + k) * row_devs][:, :CAP] for k in range(chips)], axis=1
+            [got_values[at * chips + k][:, :CAP] for k in range(chips)], axis=1
         )
         tags = jnp.broadcast_to(tags, (8, block)).astype(jnp.bfloat16)
         moment[...] += jnp.dot(tags, rows, preferred_element_type=jnp.float32)
@@ -243,7 +233,7 @@
     def part(i, k):
         cols = columns(k)
         return push(
-            halves.at[i, :, cols], right.at[i, :, cols], tile_send.at[i, k], tile_recv.at[i, k], partner,
+            halves.at[i, :, cols], right.at[i, :, cols], tile_send, tile_recv.at[i, k // 2], partner,
         )
 
     for sub in range(subs):
@@ -314,18 +304,17 @@
     @pl.when(r == 0)
     def _():
         lend.wait_send()
-        for i in range(2):
-            for k in range(tiles):
-                part(i, k).wait_send()
+        push(halves, right, tile_send, tile_recv.at[0, 0], partner).wait_send()
 
     @pl.when(r == 1)
     def _():
         lend.wait_recv()
         b_ref[...] += b_got[...] + apply(gain, b_got[...])
         def compose_high(k, _):
-            for inner in range(wide // tile):
-                part(0, k * (wide // tile) + inner).wait_recv()
             cols = span(k)
+            pltpu.make_async_copy(
+                right.at[0, :, cols], right.at[0, :, cols], tile_recv.at[0, k]
+            ).wait()
             high = right[0, :, cols]
             whole[:, cols] = (
                 gain[:, cols] + high.astype(jnp.float32)
@@ -337,9 +326,10 @@
         lax.fori_loop(0, width // wide, compose_high, 0)
 
         def compose_low(k, _):
-            for inner in range(wide // tile):
-                part(1, k * (wide // tile) + inner).wait_recv()
             cols = span(k)
+            pltpu.make_async_copy(
+                right.at[1, :, cols], right.at[1, :, cols], tile_recv.at[1, k]
+            ).wait()
             low = right[1, :, cols]
             whole[:, cols] += low.astype(jnp.float32) + jnp.dot(
                 halves[0], low, preferred_element_type=jnp.float32
@@ -415,19 +405,15 @@
         onward.wait_send()
         aside.wait_send()
 
-    def finish(slab, _):
-        @pl.when(slab != me)
-        def _():
-            rows, tags = copies(slab, here)
-            rows.wait_send()
-
-            @pl.when(r == 0)
-            def _():
-                tags.wait_send()
-
-        return 0
-
-    lax.fori_loop(0, slabs, finish, 0)
+    pltpu.make_async_copy(
+        sent.at[pl.ds(0, slabs - 1)], sent.at[pl.ds(0, slabs - 1)], all_sent.at[0]
+    ).wait()
+
+    @pl.when(r == 0)
+    def _():
+        pltpu.make_async_copy(
+            sent_values.at[pl.ds(0, slabs - 1)], sent_values.at[pl.ds(0, slabs - 1)], all_sent.at[1]
+        ).wait()
 
 
 def body(initial, dynamics, obs_rows, obs_values, obs_slab):
@@ -443,7 +429,7 @@
     small = pltpu.VMEM((subs, LANES), jnp.float32)
     square = pltpu.VMEM((width, width), jnp.float32)
     halves = pltpu.VMEM((2, width, width), jnp.bfloat16)
-    sems = pltpu.SemaphoreType.DMA((slabs,))
+    sems = pltpu.SemaphoreType.DMA((time_devs * CAP // 256,))
     states = pl.pallas_call(
         observer_kernel,
         out_shape=jax.ShapeDtypeStruct((2, subs // 2, LANES), jnp.float32),
@@ -456,7 +442,7 @@
             pltpu.VMEM((slabs, 1, LANES), jnp.float32),
             pltpu.VMEM((1, count), jnp.int32),
             pltpu.VMEM((time_devs * CAP, width), jnp.bfloat16),
-            pltpu.VMEM((slabs, 1, LANES), jnp.float32),
+            pltpu.VMEM((time_devs, 1, LANES), jnp.float32),
             square,
             pltpu.VMEM((width, width), jnp.bfloat16),
             pltpu.VMEM((width, 256), jnp.bfloat16),
@@ -471,14 +457,13 @@
             small,
             small,
             pltpu.VMEM((2, subs, LANES), jnp.float32),
+            pltpu.SemaphoreType.DMA((2,)),
             sems,
             sems,
-            sems,
-            sems,
-            pltpu.SemaphoreType.DMA((4,)),
-            pltpu.SemaphoreType.DMA((2,)),
-            pltpu.SemaphoreType.DMA((2, tiles)),
-            pltpu.SemaphoreType.DMA((2, tiles)),
+            pltpu.SemaphoreType.DMA((2,)),
+            pltpu.SemaphoreType.DMA((2,)),
+            pltpu.SemaphoreType.DMA,
+            pltpu.SemaphoreType.DMA((2, tiles // 2)),
             pltpu.SemaphoreType.DMA((2,)),
             pltpu.SemaphoreType.DMA((1,)),
             pltpu.SemaphoreType.DMA((2,)),

time: 85.1 us -> 83.7 us (0.984)
  Pallas kernels: 83.6 us -> 82.2 us
    pallas_call x1, Pallas kernels: 83.6 us -> 82.2 us  [body(): pl.pallas_call(observer_kernel, out_shape=jax.ShapeDtypeStruct((2, subs /...]
where the time goes in v5:
time: 83.7 us; the launch traced here: 83.5 us
  Pallas kernels  82.2 us (98%)
  local copies, waits for them, and re-layouts  1.28 us (2%)
    pallas_call x1, Pallas kernels, body(): pl.pallas_call(observer_kernel, out_shape=jax.ShapeDtypeStruct((2, subs /...  82.2 us

profile of v5, /device:TPU:29, one launch (start us, length us, event | category | flops | bytes accessed | tf_op | source)
XLA Modules:
  0.0 83.5 jit_solution(12391223293129949799)
XLA Ops:
  0.0 82.2 %observer.1 = f32[2,4,128]{2,1,0:T(4,128)} custom-call(s32[1,2048]{1,0:T(1,128)} %bitcast.8, bf16[2048,512]{1,0:T(8,128)(2,1)} %rows_hbm.1, bf16[16,128]{1,0:T(8,128)(2,1)} %bitcast.9, f32[1024,1024]{1,0:T(8,128)} %dynamics_ref.1, f32[8,128]{1,0:T(8,128)} %bitcast.10), custom_call_target="tpu_custom_call" | custom-call | tf_op jit(solution)/shard_map/observer/pallas_call | solution.py:433
  82.2 1.3 %copy.8 = f32[1,2,4,128]{3,1,2,0:T(2,128)} copy(f32[1,2,4,128]{3,2,1,0:T(4,128)} %bitcast.7) | data formatting | bytes 8192

commit v6 on v5

--- a/solution.py
+++ b/solution.py
@@ -232,8 +232,10 @@
 
     def part(i, k):
         cols = columns(k)
+        source = right if i else halves
         return push(
-            halves.at[i, :, cols], right.at[i, :, cols], tile_send, tile_recv.at[i, k // 2], partner,
+            source.at[i, :, cols], right.at[i, :, cols], tile_send,
+            tile_recv.at[i, k if i else k // 2], partner,
         )
 
     for sub in range(subs):
@@ -245,6 +247,14 @@
 
     def span(k):
         return pl.ds(pl.multiple_of(k * wide, wide), wide)
+
+    spans = width // wide
+
+    def give(k):
+        cols = span(k)
+        return push(
+            halves.at[0, :, cols], right.at[0, :, cols], tile_send, tile_recv.at[0, k], partner
+        )
 
     def settle(cols):
         moved = jnp.dot(rounded[...], dyn_high[:, cols], preferred_element_type=jnp.float32)
@@ -264,16 +274,15 @@
             return 0
 
         lax.fori_loop(0, tiles, settle_sent, 0)
-        for k in range(tiles):
-            part(1, k).start()
 
     @pl.when(r == 1)
     def _():
         def settle_kept(k, _):
             settle(span(k))
+            give(k).start()
             return 0
 
-        lax.fori_loop(0, width // wide, settle_kept, 0)
+        lax.fori_loop(0, spans, settle_kept, 0)
 
     lane = lax.broadcasted_iota(jnp.int32, (subs, LANES), 1)
     line = lax.broadcasted_iota(jnp.int32, (subs, LANES), 0)
@@ -303,6 +312,32 @@
 
     @pl.when(r == 0)
     def _():
+        def refine(j, cols):
+            deep = span(j)
+            return jnp.dot(
+                right[0, :, deep], halves[1, deep, cols], preferred_element_type=jnp.float32
+            )
+
+        for j in range(spans - 1):
+            give(j).wait_recv()
+
+            def early(k, _):
+                cols = span(k)
+                known = halves[1, :, cols].astype(jnp.float32) if j == 0 else whole[:, cols]
+                whole[:, cols] = known + refine(j, cols)
+                return 0
+
+            lax.fori_loop(0, spans, early, 0)
+
+        give(spans - 1).wait_recv()
+
+        def late(k, _):
+            cols = columns(k)
+            right[1, :, cols] = (whole[:, cols] + refine(spans - 1, cols)).astype(jnp.bfloat16)
+            part(1, k).start()
+            return 0
+
+        lax.fori_loop(0, tiles, late, 0)
         lend.wait_send()
         push(halves, right, tile_send, tile_recv.at[0, 0], partner).wait_send()
 
@@ -323,20 +358,16 @@
             )
             return 0
 
-        lax.fori_loop(0, width // wide, compose_high, 0)
+        lax.fori_loop(0, spans, compose_high, 0)
 
         def compose_low(k, _):
-            cols = span(k)
-            pltpu.make_async_copy(
-                right.at[1, :, cols], right.at[1, :, cols], tile_recv.at[1, k]
-            ).wait()
-            low = right[1, :, cols]
-            whole[:, cols] += low.astype(jnp.float32) + jnp.dot(
-                halves[0], low, preferred_element_type=jnp.float32
-            )
+            cols = columns(k)
+            part(1, k).wait_recv()
+            whole[:, cols] += right[1, :, cols].astype(jnp.float32)
             return 0
 
-        lax.fori_loop(0, width // wide, compose_low, 0)
+        lax.fori_loop(0, tiles, compose_low, 0)
+        push(halves.at[0], right.at[0], tile_send, tile_recv.at[0, 0], partner).wait_send()
 
     onward = push(went, came, pass_send.at[1], pass_recv.at[0], (after, 1))
     aside = push(went, came, pass_send.at[0], pass_recv.at[0], (after, 0))
@@ -463,7 +494,7 @@
             pltpu.SemaphoreType.DMA((2,)),
             pltpu.SemaphoreType.DMA((2,)),
             pltpu.SemaphoreType.DMA,
-            pltpu.SemaphoreType.DMA((2, tiles // 2)),
+            pltpu.SemaphoreType.DMA((2, tiles)),
             pltpu.SemaphoreType.DMA((2,)),
             pltpu.SemaphoreType.DMA((1,)),
             pltpu.SemaphoreType.DMA((2,)),

time: 83.7 us -> 83.8 us (level)
  no operation moved by 1% of the time
where the time goes in v6:
time: 83.8 us; the launch traced here: 83.5 us
  Pallas kernels  82.3 us (98%)
  local copies, waits for them, and re-layouts  1.28 us (2%)
    pallas_call x1, Pallas kernels, body(): pl.pallas_call(observer_kernel, out_shape=jax.ShapeDtypeStruct((2, subs /...  82.3 us

profile of v6, /device:TPU:29, one launch (start us, length us, event | category | flops | bytes accessed | tf_op | source)
XLA Modules:
  0.0 83.5 jit_solution(4765180720930073322)
XLA Ops:
  0.0 82.3 %observer.1 = f32[2,4,128]{2,1,0:T(4,128)} custom-call(s32[1,2048]{1,0:T(1,128)} %bitcast.8, bf16[2048,512]{1,0:T(8,128)(2,1)} %rows_hbm.1, bf16[16,128]{1,0:T(8,128)(2,1)} %bitcast.9, f32[1024,1024]{1,0:T(8,128)} %dynamics_ref.1, f32[8,128]{1,0:T(8,128)} %bitcast.10), custom_call_target="tpu_custom_call" | custom-call | tf_op jit(solution)/shard_map/observer/pallas_call | solution.py:464
  82.3 1.3 %copy.8 = f32[1,2,4,128]{3,1,2,0:T(2,128)} copy(f32[1,2,4,128]{3,2,1,0:T(4,128)} %bitcast.7) | data formatting | bytes 8192

commit v7 on v6

--- a/solution.py
+++ b/solution.py
@@ -141,8 +141,6 @@
     depth = t // 4
 
     def order(turn):
-        mixed = lax.rem(turn, 2) * column_blocks + turn // 2
-        turn = jnp.where(((t >> 1) & 1 == 0) & (turn < 2 * column_blocks), mixed, turn)
         column = turn // column_blocks
         along = jnp.where(column & 1 == 1, depth, planes - 1 - depth)
         own = along * row_devs // share

time: 83.8 us -> 83.8 us (level)
  no operation moved by 1% of the time
where the time goes in v7:
time: 83.8 us; the launch traced here: 83.5 us
  Pallas kernels  82.3 us (98%)
  local copies, waits for them, and re-layouts  1.28 us (2%)
    pallas_call x1, Pallas kernels, body(): pl.pallas_call(observer_kernel, out_shape=jax.ShapeDtypeStruct((2, subs /...  82.3 us

profile of v7, /device:TPU:29, one launch (start us, length us, event | category | flops | bytes accessed | tf_op | source)
XLA Modules:
  0.0 83.5 jit_solution(5562254942849523637)
XLA Ops:
  0.0 82.3 %observer.1 = f32[2,4,128]{2,1,0:T(4,128)} custom-call(s32[1,2048]{1,0:T(1,128)} %bitcast.8, bf16[2048,512]{1,0:T(8,128)(2,1)} %rows_hbm.1, bf16[16,128]{1,0:T(8,128)(2,1)} %bitcast.9, f32[1024,1024]{1,0:T(8,128)} %dynamics_ref.1, f32[8,128]{1,0:T(8,128)} %bitcast.10), custom_call_target="tpu_custom_call" | custom-call | tf_op jit(solution)/shard_map/observer/pallas_call | solution.py:462
  82.3 1.3 %copy.8 = f32[1,2,4,128]{3,1,2,0:T(2,128)} copy(f32[1,2,4,128]{3,2,1,0:T(4,128)} %bitcast.7) | data formatting | bytes 8192

commit v8 on v7

--- a/solution.py
+++ b/solution.py
@@ -267,11 +267,12 @@
         lend.start()
 
         def settle_sent(k, _):
-            settle(columns(k))
-            part(0, k).start()
+            settle(span(k))
+            for inner in range(wide // tile):
+                part(0, k * (wide // tile) + inner).start()
             return 0
 
-        lax.fori_loop(0, tiles, settle_sent, 0)
+        lax.fori_loop(0, spans, settle_sent, 0)
 
     @pl.when(r == 1)
     def _():

time: 83.8 us -> 83.8 us (level)
  no operation moved by 1% of the time
where the time goes in v8:
time: 83.8 us; the launch traced here: 83.5 us
  Pallas kernels  82.3 us (98%)
  local copies, waits for them, and re-layouts  1.28 us (2%)
    pallas_call x1, Pallas kernels, body(): pl.pallas_call(observer_kernel, out_shape=jax.ShapeDtypeStruct((2, subs /...  82.3 us

profile of v8, /device:TPU:29, one launch (start us, length us, event | category | flops | bytes accessed | tf_op | source)
XLA Modules:
  0.0 83.5 jit_solution(14638282485193493833)
XLA Ops:
  0.0 82.3 %observer.1 = f32[2,4,128]{2,1,0:T(4,128)} custom-call(s32[1,2048]{1,0:T(1,128)} %bitcast.8, bf16[2048,512]{1,0:T(8,128)(2,1)} %rows_hbm.1, bf16[16,128]{1,0:T(8,128)(2,1)} %bitcast.9, f32[1024,1024]{1,0:T(8,128)} %dynamics_ref.1, f32[8,128]{1,0:T(8,128)} %bitcast.10), custom_call_target="tpu_custom_call" | custom-call | tf_op jit(solution)/shard_map/observer/pallas_call | solution.py:463
  82.3 1.3 %copy.8 = f32[1,2,4,128]{3,1,2,0:T(2,128)} copy(f32[1,2,4,128]{3,2,1,0:T(4,128)} %bitcast.7) | data formatting | bytes 8192
